TPU v7x, 32 devices: a whole 2x2x4 slice. The times are simulated.
32 devices in a mesh: groups: 2 (over y), shard: 16 (over z, x, core).
Axes of the slice: x: 2, y: 2, z: 4, core: 2. Of those that a mesh axis runs over, the one named last changes fastest.
Arguments:
- query_tokens: bfloat16 [1024, 32, 128], P(('groups', 'shard')), parts along dimension 0, may hold values from -0.1875 to 0.1875
- candidates: int32 [1024, 24], P(('groups', 'shard')), parts along dimension 0, may hold values from 0 to 511, as said below
- cand_count: int32 [1024], P(('groups', 'shard')), parts along dimension 0, may hold values from 3 to 24, as said below
- placement_map: int32 [1024], P('groups'), parts along dimension 0, may hold values from 0 to 511, as said below
- passage_base: bfloat16 [1024, 128, 128], P(('groups', 'shard')), parts along dimension 0, may hold values from -6 to 6
- residual_codes: int32 [1024, 128, 128], P(('groups', 'shard')), parts along dimension 0, may hold values from 0 to 3
- passage_lengths: int32 [1024], P(('groups', 'shard')), parts along dimension 0, may hold values from 32 to 128
- bucket_weights: float32 [8], P('groups'), parts along dimension 0, may hold values from -3 to 3
Outputs:
- scores: float32 [1024, 24], P(('groups', 'shard')), parts along dimension 0
There are 2 independent parts, one for each index of `groups`. A program takes and returns all parts, laid end to end along the dimension named above; each array names one. Nothing has to cross between parts.
Inputs may be any that keep to these rules, and one draw needn't show every extreme that they name: In row q the first cand_count[q] entries are distinct passage ids; the devices that store them (device placement_map[id] // 32 of the shard axis) are at most 3, and one device stores at most 8 of them. Of the 32 queries of one device, one storing device (the same for all devices) holds candidates of exactly 9, and every other storing device holds candidates of at most 6. Entries at or beyond cand_count[q] are arbitrary ids. `cand_count`: entries of candidates at or beyond this count are not scored. A permutation: passage id p is row placement_map[p] of the passage store.
All inputs are finite; a program needn't handle non-finite values.
Results may differ from a plain program's by a relative error of at most 0.0003.
Values may be sent and summed in bfloat16 or wider, within the bound.
A program may use at most 64 MiB of HBM per device.

v0:
```python
import jax
import jax.numpy as jnp
from jax import lax
from jax.sharding import PartitionSpec as P

OWNERS_Q = 3
CPQ = 8
epsilon = 1e-06
negative = -1e30


def decode(bases, code_ids, levels):
    residual = jnp.zeros(bases.shape, jnp.float32)
    for bucket in range(4):
        residual = residual + jnp.where(code_ids == bucket, levels[bucket], 0.0)
    summed = bases.astype(jnp.float32) + residual
    inverse_norm = lax.rsqrt(jnp.sum(summed * summed, axis=-1, keepdims=True) + epsilon)
    return (summed * inverse_norm).astype(jnp.bfloat16)


def score_block(query_rows, token_rows, lengths):
    similarity_scores = jnp.einsum(
        "mqd,mkpd->mqkp", query_rows, token_rows, preferred_element_type=jnp.float32
    )
    inside = (
        jnp.arange(token_rows.shape[2], dtype=jnp.int32)[None, None, None, :]
        < lengths[:, None, :, None]
    )
    maxima = jnp.max(jnp.where(inside, similarity_scores, negative), axis=3)
    return jnp.sum(maxima, axis=1)


def score_slots(query_rows, wanted, decoded, lengths):
    item_count = query_rows.shape[0]
    group_size = 16
    padding = -item_count % group_size
    wanted = jnp.maximum(wanted, 0)
    blocks = (item_count + padding) // group_size

    def one_block(bundle):
        query_part, row_part = bundle
        return score_block(query_part, decoded[row_part], lengths[row_part])

    result = lax.map(
        one_block,
        (
            query_rows.reshape(blocks, group_size, query_rows.shape[1], query_rows.shape[2]),
            wanted.reshape(blocks, group_size, wanted.shape[1]),
        ),
    )
    return result.reshape(blocks * group_size, wanted.shape[1])


def pack(present, holder, capacity, query_tokens):
    present_int = present.astype(jnp.int32)
    slot_of = jnp.cumsum(present_int, axis=0) - present_int
    selection_mask = present.T[:, None, :] & (
        slot_of.T[:, None, :] == jnp.arange(capacity, dtype=jnp.int32)[None, :, None]
    )
    outgoing = jnp.einsum(
        "ksq,qtd->kstd",
        selection_mask.astype(jnp.bfloat16),
        query_tokens,
        preferred_element_type=jnp.float32,
    ).astype(jnp.bfloat16)
    target = (
        jnp.sum(
            selection_mask[:, :, :, None].astype(jnp.int32)
            * (jnp.transpose(holder, (1, 0, 2))[:, None, :, :] + 1),
            axis=2,
        )
        - 1
    )
    return (outgoing, target, slot_of)


def local(
    query_tokens,
    candidates,
    cand_count,
    placement_map,
    passage_base,
    residual_codes,
    passage_lengths,
    bucket_weights,
):
    device_count = lax.axis_size("shard")
    query_count, slot_count = candidates.shape
    store_rows = passage_base.shape[0]
    hot_cap = query_count * OWNERS_Q // device_count + 3
    decoded = decode(passage_base, residual_codes, bucket_weights)
    usable = jnp.arange(slot_count, dtype=jnp.int32)[None, :] < cand_count[:, None]
    stored = placement_map[candidates]
    holders = stored // store_rows
    local_row = stored % store_rows
    shared = usable[:, :, None] & usable[:, None, :] & (holders[:, :, None] == holders[:, None, :])
    preceding_total = (
        jnp.arange(slot_count, dtype=jnp.int32)[None, :]
        < jnp.arange(slot_count, dtype=jnp.int32)[:, None]
    )
    within = jnp.sum((shared & preceding_total[None, :, :]).astype(jnp.int32), axis=2)
    owner_ids = jnp.arange(device_count, dtype=jnp.int32)
    matches = usable[:, :, None] & (holders[:, :, None] == owner_ids[None, None, :])
    present = jnp.any(matches, axis=1)
    rank_ids = jnp.arange(CPQ, dtype=jnp.int32)
    holder = (
        jnp.sum(
            jnp.where(
                matches[:, :, :, None]
                & (within[:, :, None, None] == rank_ids[None, None, None, :]),
                local_row[:, :, None, None] + 1,
                0,
            ),
            axis=1,
        )
        - 1
    )
    outgoing, target, slot_of = pack(present, holder, hot_cap, query_tokens)
    queries_in = lax.all_to_all(outgoing, "shard", split_axis=0, concat_axis=0, tiled=True)
    rows_in = lax.all_to_all(
        target.astype(jnp.bfloat16), "shard", split_axis=0, concat_axis=0, tiled=True
    )
    senders = rows_in.shape[0]
    slots_in = rows_in.shape[1]
    flat_queries = queries_in.reshape(senders * slots_in, queries_in.shape[2], queries_in.shape[3])
    row_list_flat = rows_in.astype(jnp.int32).reshape(senders * slots_in, rows_in.shape[2])
    visited = score_slots(flat_queries, row_list_flat, decoded, passage_lengths).reshape(
        senders, slots_in, rows_in.shape[2]
    )
    returned = lax.all_to_all(visited, "shard", split_axis=0, concat_axis=0, tiled=True)
    flattened = returned.reshape(-1)
    pick_slot = jnp.take_along_axis(slot_of, jnp.clip(holders, 0, device_count - 1), axis=1)
    position = holders * (hot_cap * CPQ) + pick_slot * CPQ + within
    result = jnp.take(flattened, position, mode="clip")
    return jnp.where(usable, result, 0.0)


def solution(mesh):
    return jax.shard_map(
        local,
        mesh=mesh,
        in_specs=(
            P(("groups", "shard"), None, None),
            P(("groups", "shard"), None),
            P(("groups", "shard")),
            P("groups"),
            P(("groups", "shard"), None, None),
            P(("groups", "shard"), None, None),
            P(("groups", "shard")),
            P("groups"),
        ),
        out_specs=P(("groups", "shard"), None),
        check_vma=False,
    )
```

profile of v0, /device:TPU:0, one launch (start us, length us, event | category | flops | bytes accessed | tf_op | source)
XLA Modules:
  0.0 154.1 jit_solution(14491903596649840008)
XLA Ops:
  0.0 0.7 iota_compare_fusion.4
  0.8 0.7 compare_select_fusion.2
  1.8 5.0 %gather_fusion.2 = s32[768]{0:T(1024)S(1)} fusion(s32[512]{0:T(512)S(1)} %copy-done, s32[1024]{0:T(1024)S(1)} %pad_clamp_fusion.2), kind=kCustom, calls=%fused_computation.2 | custom fusion | bytes 9216 | tf_op jit(solution)/shard_map/gather | solution.py:93
  7.0 0.2 convert_reduce_fusion
  7.5 0.3 select_reduce_fusion.1
  7.8 2.5 %multiply_reduce_fusion.1 = s32[16,9,8]{2,1,0:T(8,128)S(1)} fusion(s32[16,32,8]{1,2,0:T(8,128)S(1)} %bitcast.58, s32[16,9,32]{2,1,0:T(8,128)S(1)} %copy.110), kind=kLoop, calls=%fused_computation.18 | loop fusion | flops 72576 | bytes 39424 | tf_op jit(solution)/shard_map/reduce_sum | solution.py:67
  10.3 0.1 copy.113
  10.5 0.7 copy.114
  11.2 7.4 %all-to-all-start = ((bf16[16,9,8]{1,2,0:T(8,128)(2,1)}), bf16[16,9,8]{1,2,0:T(8,128)(2,1)S(1)}, u32[]{:S(2)}, u32[]{:S(2)}) async-start(bf16[16,9,8]{1,2,0:T(8,128)(2,1)} %copy.114), calls=%async_computation | async-start | bytes 65536 | tf_op jit(solution)/shard_map/all_to_all | solution.py:120
  18.6 0.5 convolution_convert_fusion
  19.1 1.3 copy.118
  20.4 4.9 %all-to-all-done = bf16[16,9,8]{1,2,0:T(8,128)(2,1)S(1)} async-done(((bf16[16,9,8]{1,2,0:T(8,128)(2,1)}), bf16[16,9,8]{1,2,0:T(8,128)(2,1)S(1)}, u32[]{:S(2)}, u32[]{:S(2)}) %all-to-all-start) | async-done | bytes 2336 | tf_op jit(solution)/shard_map/all_to_all | solution.py:120
  25.2 4.4 %all-to-all-start.1 = ((bf16[16,9,32,128]{3,2,1,0:T(8,128)(2,1)}), bf16[16,9,32,128]{3,2,1,0:T(8,128)(2,1)}, u32[]{:S(2)}, u32[]{:S(2)}) async-start(bf16[16,9,32,128]{3,2,1,0:T(8,128)(2,1)} %copy.118), calls=%async_computation.1 | async-start | bytes 2359296 | tf_op jit(solution)/shard_map/all_to_all | solution.py:119
  30.0 5.1 %gather_fusion.4 = s32[768]{0:T(1024)S(1)} fusion(s32[32,16]{1,0:T(8,128)S(1)} %convert_subtract_fusion, s32[768]{0:T(1024)S(1)} %reshape.292), kind=kCustom, calls=%fused_computation.4 | custom fusion | bytes 12288 | tf_op jit(solution)/shard_map/jit(take_along_axis)/gather | solution.py:132
  35.5 0.6 fusion.18
  36.2 4.8 %multiply_reduce_fusion = f32[32,128]{1,0:T(8,128)S(1)} fusion(f32[]{:T(128)} %bitcast.17, s32[32,128,128]{2,1,0:T(8,128)S(1)} %copy-done.2, f32[]{:T(128)} %bitcast.16, f32[]{:T(128)} %bitcast.15, f32[]{:T(128)} %bitcast.14, bf16[32,128,128]{2,1,0:T(8,128)(2,1)} %param.14), kind=kLoop, calls=%fused_computation.14 | loop fusion | flops 7860224 | bytes 3162128 | tf_op jit(solution)/shard_map/reduce_sum | solution.py:17
  41.0 4.6 %multiply_convert_fusion = bf16[32,128,128]{2,1,0:T(8,128)(2,1)S(1)} fusion(f32[32,128]{1,0:T(8,128)S(1)} %add_rsqrt_fusion, f32[]{:T(128)} %bitcast.17, s32[32,128,128]{2,1,0:T(8,128)S(1)} %copy-done.2, f32[]{:T(128)} %bitcast.16, f32[]{:T(128)} %bitcast.15, f32[]{:T(128)} %bitcast.14, bf16[32,128,128]{2,1,0:T(8,128)(2,1)} %param.14), kind=kLoop, calls=%fused_computation.13 | loop fusion | flops 7864320 | bytes 4210704 | tf_op jit(solution)/shard_map/convert_element_type | solution.py:18
  45.6 0.1 copy.115
  45.8 0.1 copy.116
  45.9 0.1 max.16
  46.0 8.7 %all-to-all-done.1 = bf16[16,9,32,128]{3,2,1,0:T(8,128)(2,1)} async-done(((bf16[16,9,32,128]{3,2,1,0:T(8,128)(2,1)}), bf16[16,9,32,128]{3,2,1,0:T(8,128)(2,1)}, u32[]{:S(2)}, u32[]{:S(2)}) %all-to-all-start.1) | async-done | bytes 1179680 | tf_op jit(solution)/shard_map/all_to_all | solution.py:119
  54.7 78.7 %while.10 = (s32[]{:T(128)}, f32[9,16,8]{1,0,2:T(8,128)S(1)}, s32[9,16,8]{1,0,2:T(8,128)S(1)}, s32[32]{0:T(128)S(1)}, bf16[9,16,32,128]{3,2,1,0:T(8,128)(2,1)}, ...) while((s32[]{:T(128)}, f32[9,16,8]{1,0,2:T(8,128)S(1)}, ...), condition=%wide.region_9.10_spmd, body=%wide.region_6.9_spmd.sunk | while | flops 135283968 | bytes 12794485 | solution.py:44
  54.9 1.2 gather_fusion.1
  56.2 0.1 iota_compare_fusion.7
  56.3 3.0 %gather_fusion = bf16[128,128,128]{2,1,0:T(8,128)(2,1)} fusion(bf16[32,128,128]{2,1,0:T(8,128)(2,1)S(1)} %get-tuple-element.148, s32[1024]{0:T(1024)S(1)} %pad_clamp_fusion.4), kind=kCustom, calls=%fused_computation.1.clone.1 | custom fusion | bytes 8389120 | tf_op jit(solution)/shard_map/while/body/eval_jaxpr/gather | solution.py:42
  59.3 3.9 %select_reduce_fusion.3 = f32[16,32,8]{1,2,0:T(8,128)S(1)} fusion(bf16[16,8,128,128]{3,2,1,0:T(8,128)(2,1)} %bitcast.55, pred[16,8,128]{2,1,0:T(8,128)(4,1)S(1)} %iota_compare_fusion.7, bf16[9,16,32,128]{3,2,1,0:T(8,128)(2,1)} %get-tuple-element.147, s32[]{:T(128)S(6)} %copy.149), kind=kOutput, calls=%fused_computation.5.clone.1 | convolution fusion | flops 135262208 | bytes 4358148 | tf_op jit(solution)/shard_map/while/body/eval_jaxpr/mqd,mkpd->mqkp/dot_general | solution.py:22
  63.6 1.2 gather_fusion.1
  64.9 0.1 iota_compare_fusion.7
  65.0 3.0 %gather_fusion = bf16[128,128,128]{2,1,0:T(8,128)(2,1)} fusion(bf16[32,128,128]{2,1,0:T(8,128)(2,1)S(1)} %get-tuple-element.148, s32[1024]{0:T(1024)S(1)} %pad_clamp_fusion.4), kind=kCustom, calls=%fused_computation.1.clone.1 | custom fusion | bytes 8389120 | tf_op jit(solution)/shard_map/while/body/eval_jaxpr/gather | solution.py:42
  68.1 3.9 %select_reduce_fusion.3 = f32[16,32,8]{1,2,0:T(8,128)S(1)} fusion(bf16[16,8,128,128]{3,2,1,0:T(8,128)(2,1)} %bitcast.55, pred[16,8,128]{2,1,0:T(8,128)(4,1)S(1)} %iota_compare_fusion.7, bf16[9,16,32,128]{3,2,1,0:T(8,128)(2,1)} %get-tuple-element.147, s32[]{:T(128)S(6)} %copy.149), kind=kOutput, calls=%fused_computation.5.clone.1 | convolution fusion | flops 135262208 | bytes 4358148 | tf_op jit(solution)/shard_map/while/body/eval_jaxpr/mqd,mkpd->mqkp/dot_general | solution.py:22
  72.4 1.2 gather_fusion.1
  73.7 0.1 iota_compare_fusion.7
  73.8 3.0 %gather_fusion = bf16[128,128,128]{2,1,0:T(8,128)(2,1)} fusion(bf16[32,128,128]{2,1,0:T(8,128)(2,1)S(1)} %get-tuple-element.148, s32[1024]{0:T(1024)S(1)} %pad_clamp_fusion.4), kind=kCustom, calls=%fused_computation.1.clone.1 | custom fusion | bytes 8389120 | tf_op jit(solution)/shard_map/while/body/eval_jaxpr/gather | solution.py:42
  76.8 3.9 %select_reduce_fusion.3 = f32[16,32,8]{1,2,0:T(8,128)S(1)} fusion(bf16[16,8,128,128]{3,2,1,0:T(8,128)(2,1)} %bitcast.55, pred[16,8,128]{2,1,0:T(8,128)(4,1)S(1)} %iota_compare_fusion.7, bf16[9,16,32,128]{3,2,1,0:T(8,128)(2,1)} %get-tuple-element.147, s32[]{:T(128)S(6)} %copy.149), kind=kOutput, calls=%fused_computation.5.clone.1 | convolution fusion | flops 135262208 | bytes 4358148 | tf_op jit(solution)/shard_map/while/body/eval_jaxpr/mqd,mkpd->mqkp/dot_general | solution.py:22
  81.1 1.2 gather_fusion.1
  82.4 0.1 iota_compare_fusion.7
  82.5 3.0 %gather_fusion = bf16[128,128,128]{2,1,0:T(8,128)(2,1)} fusion(bf16[32,128,128]{2,1,0:T(8,128)(2,1)S(1)} %get-tuple-element.148, s32[1024]{0:T(1024)S(1)} %pad_clamp_fusion.4), kind=kCustom, calls=%fused_computation.1.clone.1 | custom fusion | bytes 8389120 | tf_op jit(solution)/shard_map/while/body/eval_jaxpr/gather | solution.py:42
  85.6 3.9 %select_reduce_fusion.3 = f32[16,32,8]{1,2,0:T(8,128)S(1)} fusion(bf16[16,8,128,128]{3,2,1,0:T(8,128)(2,1)} %bitcast.55, pred[16,8,128]{2,1,0:T(8,128)(4,1)S(1)} %iota_compare_fusion.7, bf16[9,16,32,128]{3,2,1,0:T(8,128)(2,1)} %get-tuple-element.147, s32[]{:T(128)S(6)} %copy.149), kind=kOutput, calls=%fused_computation.5.clone.1 | convolution fusion | flops 135262208 | bytes 4358148 | tf_op jit(solution)/shard_map/while/body/eval_jaxpr/mqd,mkpd->mqkp/dot_general | solution.py:22
  89.9 1.2 gather_fusion.1
  91.3 3.0 %gather_fusion = bf16[128,128,128]{2,1,0:T(8,128)(2,1)} fusion(bf16[32,128,128]{2,1,0:T(8,128)(2,1)S(1)} %get-tuple-element.148, s32[1024]{0:T(1024)S(1)} %pad_clamp_fusion.4), kind=kCustom, calls=%fused_computation.1.clone.1 | custom fusion | bytes 8389120 | tf_op jit(solution)/shard_map/while/body/eval_jaxpr/gather | solution.py:42
  94.3 3.9 %select_reduce_fusion.3 = f32[16,32,8]{1,2,0:T(8,128)S(1)} fusion(bf16[16,8,128,128]{3,2,1,0:T(8,128)(2,1)} %bitcast.55, pred[16,8,128]{2,1,0:T(8,128)(4,1)S(1)} %iota_compare_fusion.7, bf16[9,16,32,128]{3,2,1,0:T(8,128)(2,1)} %get-tuple-element.147, s32[]{:T(128)S(6)} %copy.149), kind=kOutput, calls=%fused_computation.5.clone.1 | convolution fusion | flops 135262208 | bytes 4358148 | tf_op jit(solution)/shard_map/while/body/eval_jaxpr/mqd,mkpd->mqkp/dot_general | solution.py:22
  98.6 1.2 gather_fusion.1
  99.9 0.1 iota_compare_fusion.7
  100.0 3.0 %gather_fusion = bf16[128,128,128]{2,1,0:T(8,128)(2,1)} fusion(bf16[32,128,128]{2,1,0:T(8,128)(2,1)S(1)} %get-tuple-element.148, s32[1024]{0:T(1024)S(1)} %pad_clamp_fusion.4), kind=kCustom, calls=%fused_computation.1.clone.1 | custom fusion | bytes 8389120 | tf_op jit(solution)/shard_map/while/body/eval_jaxpr/gather | solution.py:42
  103.1 3.9 %select_reduce_fusion.3 = f32[16,32,8]{1,2,0:T(8,128)S(1)} fusion(bf16[16,8,128,128]{3,2,1,0:T(8,128)(2,1)} %bitcast.55, pred[16,8,128]{2,1,0:T(8,128)(4,1)S(1)} %iota_compare_fusion.7, bf16[9,16,32,128]{3,2,1,0:T(8,128)(2,1)} %get-tuple-element.147, s32[]{:T(128)S(6)} %copy.149), kind=kOutput, calls=%fused_computation.5.clone.1 | convolution fusion | flops 135262208 | bytes 4358148 | tf_op jit(solution)/shard_map/while/body/eval_jaxpr/mqd,mkpd->mqkp/dot_general | solution.py:22
  107.4 1.2 gather_fusion.1
  108.7 0.1 iota_compare_fusion.7
  108.8 3.0 %gather_fusion = bf16[128,128,128]{2,1,0:T(8,128)(2,1)} fusion(bf16[32,128,128]{2,1,0:T(8,128)(2,1)S(1)} %get-tuple-element.148, s32[1024]{0:T(1024)S(1)} %pad_clamp_fusion.4), kind=kCustom, calls=%fused_computation.1.clone.1 | custom fusion | bytes 8389120 | tf_op jit(solution)/shard_map/while/body/eval_jaxpr/gather | solution.py:42
  111.8 3.9 %select_reduce_fusion.3 = f32[16,32,8]{1,2,0:T(8,128)S(1)} fusion(bf16[16,8,128,128]{3,2,1,0:T(8,128)(2,1)} %bitcast.55, pred[16,8,128]{2,1,0:T(8,128)(4,1)S(1)} %iota_compare_fusion.7, bf16[9,16,32,128]{3,2,1,0:T(8,128)(2,1)} %get-tuple-element.147, s32[]{:T(128)S(6)} %copy.149), kind=kOutput, calls=%fused_computation.5.clone.1 | convolution fusion | flops 135262208 | bytes 4358148 | tf_op jit(solution)/shard_map/while/body/eval_jaxpr/mqd,mkpd->mqkp/dot_general | solution.py:22
  116.1 1.2 gather_fusion.1
  117.4 0.1 iota_compare_fusion.7
  117.5 3.0 %gather_fusion = bf16[128,128,128]{2,1,0:T(8,128)(2,1)} fusion(bf16[32,128,128]{2,1,0:T(8,128)(2,1)S(1)} %get-tuple-element.148, s32[1024]{0:T(1024)S(1)} %pad_clamp_fusion.4), kind=kCustom, calls=%fused_computation.1.clone.1 | custom fusion | bytes 8389120 | tf_op jit(solution)/shard_map/while/body/eval_jaxpr/gather | solution.py:42
  120.6 3.9 %select_reduce_fusion.3 = f32[16,32,8]{1,2,0:T(8,128)S(1)} fusion(bf16[16,8,128,128]{3,2,1,0:T(8,128)(2,1)} %bitcast.55, pred[16,8,128]{2,1,0:T(8,128)(4,1)S(1)} %iota_compare_fusion.7, bf16[9,16,32,128]{3,2,1,0:T(8,128)(2,1)} %get-tuple-element.147, s32[]{:T(128)S(6)} %copy.149), kind=kOutput, calls=%fused_computation.5.clone.1 | convolution fusion | flops 135262208 | bytes 4358148 | tf_op jit(solution)/shard_map/while/body/eval_jaxpr/mqd,mkpd->mqkp/dot_general | solution.py:22
  124.9 1.2 gather_fusion.1
  126.2 0.1 iota_compare_fusion.7
  126.3 3.0 %gather_fusion = bf16[128,128,128]{2,1,0:T(8,128)(2,1)} fusion(bf16[32,128,128]{2,1,0:T(8,128)(2,1)S(1)} %get-tuple-element.148, s32[1024]{0:T(1024)S(1)} %pad_clamp_fusion.4), kind=kCustom, calls=%fused_computation.1.clone.1 | custom fusion | bytes 8389120 | tf_op jit(solution)/shard_map/while/body/eval_jaxpr/gather | solution.py:42
  129.3 3.9 %select_reduce_fusion.3 = f32[16,32,8]{1,2,0:T(8,128)S(1)} fusion(bf16[16,8,128,128]{3,2,1,0:T(8,128)(2,1)} %bitcast.55, pred[16,8,128]{2,1,0:T(8,128)(4,1)S(1)} %iota_compare_fusion.7, bf16[9,16,32,128]{3,2,1,0:T(8,128)(2,1)} %get-tuple-element.147, s32[]{:T(128)S(6)} %copy.149), kind=kOutput, calls=%fused_computation.5.clone.1 | convolution fusion | flops 135262208 | bytes 4358148 | tf_op jit(solution)/shard_map/while/body/eval_jaxpr/mqd,mkpd->mqkp/dot_general | solution.py:22
  133.5 0.6 copy.121
  134.2 7.4 %all-to-all-start.2 = ((f32[16,9,8]{1,2,0:T(8,128)}), f32[16,9,8]{1,2,0:T(8,128)S(1)}, u32[]{:S(2)}, u32[]{:S(2)}) async-start(f32[16,9,8]{1,2,0:T(8,128)} %copy.121), calls=%async_computation.2 | async-start | bytes 131072 | tf_op jit(solution)/shard_map/all_to_all | solution.py:130
  141.6 6.9 %all-to-all-done.2 = f32[16,9,8]{1,2,0:T(8,128)S(1)} async-done(((f32[16,9,8]{1,2,0:T(8,128)}), f32[16,9,8]{1,2,0:T(8,128)S(1)}, u32[]{:S(2)}, u32[]{:S(2)}) %all-to-all-start.2) | async-done | bytes 4640 | tf_op jit(solution)/shard_map/all_to_all | solution.py:130
  148.5 0.2 copy.122
  148.6 0.1 reshape.259
  148.7 4.5 %gather_fusion.3 = f32[768]{0:T(1024)S(1)} fusion(f32[1152]{0:T(1024)S(1)} %reshape.259, s32[1024]{0:T(1024)S(1)} %pad_clamp_fusion.1), kind=kCustom, calls=%fused_computation.3 | custom fusion | bytes 9216 | tf_op jit(solution)/shard_map/jit(_take)/gather | solution.py:134
  153.4 0.7 copy.130
  (130 shorter events, 5.9 us)
Async XLA Ops:
  0.0 1.7 %copy-start = (s32[512]{0:T(512)S(1)}, s32[512]{0:T(512)}, u32[]{:S(2)}) copy-start(s32[512]{0:T(512)} %param.13) | copy-start | bytes 6148
  1.7 16.9 %copy-start.3 = (bf16[32,32,128]{2,1,0:T(8,128)(2,1)S(1)}, bf16[32,32,128]{2,1,0:T(8,128)(2,1)}, u32[]{:S(2)}) copy-start(bf16[32,32,128]{2,1,0:T(8,128)(2,1)} %param.10) | copy-start | bytes 786436
  11.2 14.0 %all-to-all-start = ((bf16[16,9,8]{1,2,0:T(8,128)(2,1)}), bf16[16,9,8]{1,2,0:T(8,128)(2,1)S(1)}, u32[]{:S(2)}, u32[]{:S(2)}) async-start(bf16[16,9,8]{1,2,0:T(8,128)(2,1)} %copy.114), calls=%async_computation | async-start | bytes 65536 | tf_op jit(solution)/shard_map/all_to_all | solution.py:120
  25.2 29.5 %all-to-all-start.1 = ((bf16[16,9,32,128]{3,2,1,0:T(8,128)(2,1)}), bf16[16,9,32,128]{3,2,1,0:T(8,128)(2,1)}, u32[]{:S(2)}, u32[]{:S(2)}) async-start(bf16[16,9,32,128]{3,2,1,0:T(8,128)(2,1)} %copy.118), calls=%async_computation.1 | async-start | bytes 2359296 | tf_op jit(solution)/shard_map/all_to_all | solution.py:119
  30.0 5.5 %copy-start.4 = (f32[4]{0:T(128)S(1)}, f32[4]{0:T(128)}, u32[]{:S(2)}) copy-start(f32[4]{0:T(128)} %param.17) | copy-start | bytes 52
  30.0 6.2 %copy-start.2 = (s32[32,128,128]{2,1,0:T(8,128)S(1)}, s32[32,128,128]{2,1,0:T(8,128)}, u32[]{:S(2)}) copy-start(s32[32,128,128]{2,1,0:T(8,128)} %param.15) | copy-start | bytes 6291460
  41.0 13.7 %copy-start.1 = (s32[32]{0:T(128)S(1)}, s32[32]{0:T(128)}, u32[]{:S(2)}) copy-start(s32[32]{0:T(128)} %param.16) | copy-start | bytes 388
  134.2 14.3 %all-to-all-start.2 = ((f32[16,9,8]{1,2,0:T(8,128)}), f32[16,9,8]{1,2,0:T(8,128)S(1)}, u32[]{:S(2)}, u32[]{:S(2)}) async-start(f32[16,9,8]{1,2,0:T(8,128)} %copy.121), calls=%async_computation.2 | async-start | bytes 131072 | tf_op jit(solution)/shard_map/all_to_all | solution.py:130
  148.7 4.6 %copy-start.5 = (s32[32]{0:T(128)S(1)}, s32[32]{0:T(128)}, u32[]{:S(2)}) copy-start(s32[32]{0:T(128)} %param.12) | copy-start | bytes 388
where the time goes:
time: 155 us; the launch traced here: 154 us
  local copies, waits for them, and re-layouts  62 us (40%)
  matrix products  35.5 us (23%)
  waiting for transfers between devices  20.4 us (13%)
  starting transfers between devices  19.2 us (12%)
  other arithmetic  16 us (10%)
    gather x27, local copies, waits for them, and re-layouts, one_block(): return score_block(query_part, decoded[row_part], lengths[row_part])  38.8 us
    dot_general x9, matrix products, score_block(): jnp.einsum('mqd,mkpd->mqkp', query_rows, token_rows, preferred_element_ty...  35 us
    all_to_all x1, waiting for transfers between devices, local(): lax.all_to_all(outgoing, 'shard', split_axis=0, concat_axis=0, tiled=True)  8.68 us
    all_to_all x1, starting transfers between devices, local(): lax.all_to_all(visited, 'shard', split_axis=0, concat_axis=0, tiled=True)  7.39 us
    all_to_all x1, starting transfers between devices, local(): lax.all_to_all(target.astype(jnp.bfloat16), 'shard', split_axis=0, concat...  7.39 us
    all_to_all x1, waiting for transfers between devices, local(): lax.all_to_all(visited, 'shard', split_axis=0, concat_axis=0, tiled=True)  6.88 us
    gather x5, local copies, waits for them, and re-layouts, local(): jnp.take_along_axis(slot_of, jnp.clip(holders, 0, device_count - 1), axis=1)  5.46 us
    gather x5, local copies, waits for them, and re-layouts, local(): stored = placement_map[candidates]  5.3 us
  transfers between devices with their start and end apart: 3, of which 3 were waited for; matrix products, arithmetic and copies ran while one was open for 12% of the time, Pallas kernels for 0%

commit v1 on v0

--- a/solution.py
+++ b/solution.py
@@ -7,6 +7,28 @@
 CPQ = 8
 epsilon = 1e-06
 negative = -1e30
+
+
+def in_blocks(x, dim, size):
+    before, after = (x.shape[:dim], x.shape[dim + 1 :])
+    return jnp.moveaxis(x.reshape(*before, size, -1, *after), dim, 0)
+
+
+def joined_along(blocks, dim):
+    dims = list(blocks.shape[1:])
+    dims[dim] *= blocks.shape[0]
+    return jnp.moveaxis(blocks, 0, dim).reshape(dims)
+
+
+def pairwise_exchange(x, axis, split_dim, concat_dim):
+    peers, index = (lax.axis_size(axis), lax.axis_index(axis))
+    blocks = in_blocks(x, split_dim, peers)
+    finished = [blocks[index]]
+    for step in range(1, peers):
+        sent = blocks[index ^ step]
+        finished.append(lax.ppermute(sent, axis, [(i, i ^ step) for i in range(peers)]))
+    blocks = jnp.stack(finished)[index ^ jnp.arange(peers)]
+    return joined_along(blocks, concat_dim)
 
 
 def decode(bases, code_ids, levels):
@@ -116,7 +138,7 @@
         - 1
     )
     outgoing, target, slot_of = pack(present, holder, hot_cap, query_tokens)
-    queries_in = lax.all_to_all(outgoing, "shard", split_axis=0, concat_axis=0, tiled=True)
+    queries_in = pairwise_exchange(outgoing, "shard", 0, 0)
     rows_in = lax.all_to_all(
         target.astype(jnp.bfloat16), "shard", split_axis=0, concat_axis=0, tiled=True
     )

time: 155 us -> 238 us (1.54)
  waiting for transfers between devices: 20.4 us -> 72.9 us
  local copies, waits for them, and re-layouts: 62 us -> 83.6 us
  starting transfers between devices: 19.2 us -> 27.7 us
    ppermute x0 -> x15, waiting for transfers between devices: none -> 66 us  [pairwise_exchange(): lax.ppermute(sent, axis, [(i, i ^ step) for i in range(peers)])]
    ppermute x0 -> x15, starting transfers between devices: none -> 16.8 us  [pairwise_exchange(): lax.ppermute(sent, axis, [(i, i ^ step) for i in range(peers)])]
    dynamic_update_slice x9, local copies, waits for them, and re-layouts: 0.26 us -> 12.5 us  [score_slots(): lax.map(one_block, (query_rows.reshape(blocks, group_size, query_rows.sha...]
    all_to_all x1 -> x0, waiting for transfers between devices: 8.68 us -> none  [local(): lax.all_to_all(outgoing, 'shard', split_axis=0, concat_axis=0, tiled=True)]
    all_to_all x1, waiting for transfers between devices: 4.85 us -> 0.01 us  [local(): lax.all_to_all(target.astype(jnp.bfloat16), 'shard', split_axis=0, concat...]
    all_to_all x1 -> x0, starting transfers between devices: 4.39 us -> none  [local(): lax.all_to_all(outgoing, 'shard', split_axis=0, concat_axis=0, tiled=True)]
    unnamed x12 -> x43, local copies, waits for them, and re-layouts: 0.04 us -> 4 us
    squeeze x0 -> x1, local copies, waits for them, and re-layouts: none -> 3.94 us  [pairwise_exchange(): sent = blocks[index ^ step]]
  transfers between devices with their start and end apart: 3 -> 17, of which waited for: 3 -> 11; matrix products, arithmetic and copies ran while one was open for 12% -> 10% of each run, Pallas kernels for 0% -> 0%
where the time goes in v1:
time: 238 us; the launch traced here: 236 us
  local copies, waits for them, and re-layouts  83.6 us (35%)
  waiting for transfers between devices  72.9 us (31%)
  matrix products  34.8 us (15%)
  starting transfers between devices  27.7 us (12%)
  other arithmetic  16 us (7%)
    ppermute x15, waiting for transfers between devices, pairwise_exchange(): lax.ppermute(sent, axis, [(i, i ^ step) for i in range(peers)])  66 us
    gather x27, local copies, waits for them, and re-layouts, one_block(): return score_block(query_part, decoded[row_part], lengths[row_part])  39 us
    dot_general x9, matrix products, score_block(): jnp.einsum('mqd,mkpd->mqkp', query_rows, token_rows, preferred_element_ty...  34.3 us
    ppermute x15, starting transfers between devices, pairwise_exchange(): lax.ppermute(sent, axis, [(i, i ^ step) for i in range(peers)])  16.8 us
    dynamic_update_slice x9, local copies, waits for them, and re-layouts, score_slots(): lax.map(one_block, (query_rows.reshape(blocks, group_size, query_rows.sha...  12.5 us
    all_to_all x1, starting transfers between devices, local(): lax.all_to_all(target.astype(jnp.bfloat16), 'shard', split_axis=0, concat...  7.39 us
    all_to_all x1, waiting for transfers between devices, local(): lax.all_to_all(visited, 'shard', split_axis=0, concat_axis=0, tiled=True)  6.85 us
    gather x5, local copies, waits for them, and re-layouts, local(): jnp.take_along_axis(slot_of, jnp.clip(holders, 0, device_count - 1), axis=1)  5.46 us
  transfers between devices with their start and end apart: 17, of which 11 were waited for; matrix products, arithmetic and copies ran while one was open for 10% of the time, Pallas kernels for 0%

profile of v1, /device:TPU:0, one launch (start us, length us, event | category | flops | bytes accessed | tf_op | source)
XLA Modules:
  0.0 236.0 jit_solution(537959871928346469)
XLA Ops:
  1.7 5.0 %gather_fusion.2 = s32[768]{0:T(1024)S(1)} fusion(s32[512]{0:T(512)S(1)} %copy-done, s32[1024]{0:T(1024)S(1)} %pad_clamp_fusion.3), kind=kCustom, calls=%fused_computation.2 | custom fusion | bytes 9216 | tf_op jit(solution)/shard_map/gather | solution.py:115
  7.8 2.5 %multiply_reduce_fusion.1 = s32[16,9,8]{2,1,0:T(8,128)S(1)} fusion(s32[16,32,8]{1,2,0:T(8,128)S(1)} %bitcast.95, s32[16,9,32]{2,1,0:T(8,128)S(1)} %copy.379), kind=kLoop, calls=%fused_computation.19 | loop fusion | flops 72576 | bytes 39424 | tf_op jit(solution)/shard_map/reduce_sum | solution.py:89
  11.2 7.4 %all-to-all-start = ((bf16[16,9,8]{1,2,0:T(8,128)(2,1)}), bf16[16,9,8]{1,2,0:T(8,128)(2,1)S(1)}, u32[]{:S(2)}, u32[]{:S(2)}) async-start(bf16[16,9,8]{1,2,0:T(8,128)(2,1)} %copy.383), calls=%async_computation | async-start | bytes 65536 | tf_op jit(solution)/shard_map/all_to_all | solution.py:142
  19.2 3.9 %constant_dynamic-slice_fusion.1 = (bf16[1,9,32,128]{3,0,2,1:T(2,128)(2,1)}, bf16[1,9,32,128]{3,0,2,1:T(2,128)(2,1)}, bf16[1,9,32,128]{3,0,2,1:T(2,128)(2,1)}, b...) fusion(bf16[16,9,32,128]{3,0,2,1:T(8,128)(2,1)S(1)} %convolutio, ...), kind=kLoop, calls=%fused_computation.79 | loop fusion | bytes 2359360 | tf_op jit(solution)/shard_map/squeeze | solution.py:28
  23.2 4.3 %collective-permute-start.14 = (bf16[1,9,32,128]{3,0,2,1:T(2,128)(2,1)}, bf16[1,9,32,128]{3,0,2,1:T(2,128)(2,1)}, u32[]{:S(2)}, u32[]{:S(2)}) collective-permute-start(bf16[1,9,32,128]{3,0,2,1:T(2,128)(2,1)} %get-tuple-element.164), channel_id=1, source_target_pairs={{0,15},{1,14},{2,13},{3,12},{4,11},{5,10},{6,9},{7,8},{8,7},{9,6},... | collective-permute-start | bytes 221192 | tf_op jit(solution)/shard_map/ppermute | solution.py:29
  27.9 3.2 %collective-permute-start.12 = (bf16[1,9,32,128]{3,0,2,1:T(2,128)(2,1)}, bf16[1,9,32,128]{3,0,2,1:T(2,128)(2,1)}, u32[]{:S(2)}, u32[]{:S(2)}) collective-permute-start(bf16[1,9,32,128]{3,0,2,1:T(2,128)(2,1)} %get-tuple-element.166), channel_id=1, source_target_pairs={{0,13},{1,12},{2,15},{3,14},{4,9},{5,8},{6,11},{7,10},{8,5},{9,4},... | collective-permute-start | bytes 221192 | tf_op jit(solution)/shard_map/ppermute | solution.py:29
  32.5 4.8 %multiply_reduce_fusion = f32[32,128]{1,0:T(8,128)S(1)} fusion(f32[]{:T(128)} %bitcast.19, s32[32,128,128]{2,1,0:T(8,128)S(1)} %copy-done.2, f32[]{:T(128)} %bitcast.18, f32[]{:T(128)} %bitcast.17, f32[]{:T(128)} %bitcast.16, bf16[32,128,128]{2,1,0:T(8,128)(2,1)} %param.14), kind=kLoop, calls=%fused_computation.15 | loop fusion | flops 7860224 | bytes 3162128 | tf_op jit(solution)/shard_map/reduce_sum | solution.py:39
  37.3 5.1 %gather_fusion.5 = s32[768]{0:T(1024)S(1)} fusion(s32[32,16]{1,0:T(8,128)S(1)} %convert_subtract_fusion, s32[768]{0:T(1024)S(1)} %reshape.350), kind=kCustom, calls=%fused_computation.5 | custom fusion | bytes 12288 | tf_op jit(solution)/shard_map/jit(take_along_axis)/gather | solution.py:154
  42.7 4.6 %multiply_convert_fusion = bf16[32,128,128]{2,1,0:T(8,128)(2,1)S(1)} fusion(f32[32,128]{1,0:T(8,128)S(1)} %add_rsqrt_fusion, f32[]{:T(128)} %bitcast.19, s32[32,128,128]{2,1,0:T(8,128)S(1)} %copy-done.2, f32[]{:T(128)} %bitcast.18, f32[]{:T(128)} %bitcast.17, f32[]{:T(128)} %bitcast.16, bf16[32,128,128]{2,1,0:T(8,128)(2,1)} %param.14), kind=kLoop, calls=%fused_computation.14 | loop fusion | flops 7864320 | bytes 4210704 | tf_op jit(solution)/shard_map/convert_element_type | solution.py:40
  48.0 1.7 collective-permute-start.1
  50.6 3.7 %collective-permute-done.1 = bf16[1,9,32,128]{3,0,2,1:T(2,128)(2,1)S(1)} collective-permute-done((bf16[1,9,32,128]{3,0,2,1:T(2,128)(2,1)}, bf16[1,9,32,128]{3,0,2,1:T(2,128)(2,1)S(1)}, u32[]{:S(2)}, u32[]{:S(2)}) %collective-permute-start.1) | collective-permute-done | bytes 73760 | tf_op jit(solution)/shard_map/ppermute | solution.py:29
  55.2 5.2 %collective-permute-done.2 = bf16[1,9,32,128]{3,0,2,1:T(2,128)(2,1)S(1)} collective-permute-done((bf16[1,9,32,128]{3,0,2,1:T(2,128)(2,1)}, bf16[1,9,32,128]{3,0,2,1:T(2,128)(2,1)S(1)}, u32[]{:S(2)}, u32[]{:S(2)}) %collective-permute-start.2) | collective-permute-done | bytes 73760 | tf_op jit(solution)/shard_map/ppermute | solution.py:29
  60.4 6.1 %collective-permute-done.3 = bf16[1,9,32,128]{3,0,2,1:T(2,128)(2,1)S(1)} collective-permute-done((bf16[1,9,32,128]{3,0,2,1:T(2,128)(2,1)}, bf16[1,9,32,128]{3,0,2,1:T(2,128)(2,1)S(1)}, u32[]{:S(2)}, u32[]{:S(2)}) %collective-permute-start.3) | collective-permute-done | bytes 73760 | tf_op jit(solution)/shard_map/ppermute | solution.py:29
  66.5 5.6 %collective-permute-done.4 = bf16[1,9,32,128]{3,0,2,1:T(2,128)(2,1)S(1)} collective-permute-done((bf16[1,9,32,128]{3,0,2,1:T(2,128)(2,1)S(1)}, bf16[1,9,32,128]{3,0,2,1:T(2,128)(2,1)S(1)}, u32[]{:S(2)}, u32[]{:S(2)}) %collective-permute-start.4) | collective-permute-done | bytes 73760 | tf_op jit(solution)/shard_map/ppermute | solution.py:29
  72.0 1.5 collective-permute-start.5
  73.5 4.7 %collective-permute-done.5 = bf16[1,9,32,128]{3,0,2,1:T(2,128)(2,1)S(1)} collective-permute-done((bf16[1,9,32,128]{3,0,2,1:T(2,128)(2,1)S(1)}, bf16[1,9,32,128]{3,0,2,1:T(2,128)(2,1)S(1)}, u32[]{:S(2)}, u32[]{:S(2)}) %collective-permute-start.5) | collective-permute-done | bytes 73760 | tf_op jit(solution)/shard_map/ppermute | solution.py:29
  79.2 5.8 %collective-permute-done.6 = bf16[1,9,32,128]{3,0,2,1:T(2,128)(2,1)S(1)} collective-permute-done((bf16[1,9,32,128]{3,0,2,1:T(2,128)(2,1)S(1)}, bf16[1,9,32,128]{3,0,2,1:T(2,128)(2,1)S(1)}, u32[]{:S(2)}, u32[]{:S(2)}) %collective-permute-start.6) | collective-permute-done | bytes 73760 | tf_op jit(solution)/shard_map/ppermute | solution.py:29
  85.0 3.2 %collective-permute-start.7 = (bf16[1,9,32,128]{3,0,2,1:T(2,128)(2,1)S(1)}, bf16[1,9,32,128]{3,0,2,1:T(2,128)(2,1)S(1)}, u32[]{:S(2)}, u32[]{:S(2)}) collective-permute-start(bf16[1,9,32,128]{3,0,2,1:T(2,128)(2,1)S(1)} %copy-done.8), channel_id=1, source_target_pairs={{0,8},{1,9},{2,10},{3,11},{4,12},{5,13},{6,14},{7,15},{8,0},{9,1},... | collective-permute-start | bytes 221192 | tf_op jit(solution)/shard_map/ppermute | solution.py:29
  88.2 6.4 %collective-permute-done.7 = bf16[1,9,32,128]{3,0,2,1:T(2,128)(2,1)S(1)} collective-permute-done((bf16[1,9,32,128]{3,0,2,1:T(2,128)(2,1)S(1)}, bf16[1,9,32,128]{3,0,2,1:T(2,128)(2,1)S(1)}, u32[]{:S(2)}, u32[]{:S(2)}) %collective-permute-start.7) | collective-permute-done | bytes 73760 | tf_op jit(solution)/shard_map/ppermute | solution.py:29
  94.7 9.4 %collective-permute-done.8 = bf16[1,9,32,128]{3,0,2,1:T(2,128)(2,1)S(1)} collective-permute-done((bf16[1,9,32,128]{3,0,2,1:T(2,128)(2,1)S(1)}, bf16[1,9,32,128]{3,0,2,1:T(2,128)(2,1)S(1)}, u32[]{:S(2)}, u32[]{:S(2)}) %collective-permute-start.8) | collective-permute-done | bytes 73760 | tf_op jit(solution)/shard_map/ppermute | solution.py:29
  104.4 8.8 %collective-permute-done.9 = bf16[1,9,32,128]{3,0,2,1:T(2,128)(2,1)S(1)} collective-permute-done((bf16[1,9,32,128]{3,0,2,1:T(2,128)(2,1)S(1)}, bf16[1,9,32,128]{3,0,2,1:T(2,128)(2,1)S(1)}, u32[]{:S(2)}, u32[]{:S(2)}) %collective-permute-start.9) | collective-permute-done | bytes 73760 | tf_op jit(solution)/shard_map/ppermute | solution.py:29
  113.3 10.3 %collective-permute-done.10 = bf16[1,9,32,128]{3,0,2,1:T(2,128)(2,1)S(1)} collective-permute-done((bf16[1,9,32,128]{3,0,2,1:T(2,128)(2,1)S(1)}, bf16[1,9,32,128]{3,0,2,1:T(2,128)(2,1)S(1)}, u32[]{:S(2)}, u32[]{:S(2)}) %collective-permute-start.10) | collective-permute-done | bytes 73760 | tf_op jit(solution)/shard_map/ppermute | solution.py:29
  125.5 0.9 bitcast_dynamic-update-slice_fusion.1
  128.2 90.2 %while.10 = (s32[]{:T(128)}, f32[9,16,8]{1,0,2:T(8,128)}, s32[9,16,8]{1,0,2:T(8,128)S(1)}, s32[32]{0:T(128)S(1)}, bf16[9,16,32,128]{3,2,1,0:T(8,128)(2,1)S(1)}, ...) while((s32[]{:T(128)}, f32[9,16,8]{1,0,2:T(8,128)}, s32[9,16,8]{1,0,2:T(8,128)S(1)}, ...), condition=%wide.region_9.10_spmd, body=%wide.region_6.9_spmd.sunk | while | flops 135283968 | bytes 12794485 | solution.py:66
  128.4 1.2 gather_fusion.1
  129.8 3.0 %gather_fusion = bf16[128,128,128]{2,1,0:T(8,128)(2,1)} fusion(bf16[32,128,128]{2,1,0:T(8,128)(2,1)S(1)} %get-tuple-element.248, s32[1024]{0:T(1024)S(1)} %pad_clamp_fusion.5), kind=kCustom, calls=%fused_computation.1.clone.1 | custom fusion | bytes 8389120 | tf_op jit(solution)/shard_map/while/body/eval_jaxpr/gather | solution.py:64
  132.9 3.8 %select_reduce_fusion.3 = f32[16,32,8]{1,2,0:T(8,128)S(1)} fusion(bf16[16,8,128,128]{3,2,1,0:T(8,128)(2,1)} %bitcast.90, pred[16,8,128]{2,1,0:T(8,128)(4,1)S(1)} %iota_compare_fusion.7, bf16[9,16,32,128]{3,2,1,0:T(8,128)(2,1)S(1)} %get-tuple-element.247, s32[]{:T(128)S(6)} %copy.464), kind=kOutput, calls=%fused_computation.6.clone.1 | convolution fusion | flops 135262208 | bytes 4358148 | tf_op jit(solution)/shard_map/while/body/eval_jaxpr/mqd,mkpd->mqkp/dot_general | solution.py:44
  136.9 1.4 dynamic_update_slice.5
  138.4 1.2 gather_fusion.1
  139.9 3.0 %gather_fusion = bf16[128,128,128]{2,1,0:T(8,128)(2,1)} fusion(bf16[32,128,128]{2,1,0:T(8,128)(2,1)S(1)} %get-tuple-element.248, s32[1024]{0:T(1024)S(1)} %pad_clamp_fusion.5), kind=kCustom, calls=%fused_computation.1.clone.1 | custom fusion | bytes 8389120 | tf_op jit(solution)/shard_map/while/body/eval_jaxpr/gather | solution.py:64
  142.9 3.8 %select_reduce_fusion.3 = f32[16,32,8]{1,2,0:T(8,128)S(1)} fusion(bf16[16,8,128,128]{3,2,1,0:T(8,128)(2,1)} %bitcast.90, pred[16,8,128]{2,1,0:T(8,128)(4,1)S(1)} %iota_compare_fusion.7, bf16[9,16,32,128]{3,2,1,0:T(8,128)(2,1)S(1)} %get-tuple-element.247, s32[]{:T(128)S(6)} %copy.464), kind=kOutput, calls=%fused_computation.6.clone.1 | convolution fusion | flops 135262208 | bytes 4358148 | tf_op jit(solution)/shard_map/while/body/eval_jaxpr/mqd,mkpd->mqkp/dot_general | solution.py:44
  146.9 1.4 dynamic_update_slice.5
  148.5 1.2 gather_fusion.1
  149.9 3.0 %gather_fusion = bf16[128,128,128]{2,1,0:T(8,128)(2,1)} fusion(bf16[32,128,128]{2,1,0:T(8,128)(2,1)S(1)} %get-tuple-element.248, s32[1024]{0:T(1024)S(1)} %pad_clamp_fusion.5), kind=kCustom, calls=%fused_computation.1.clone.1 | custom fusion | bytes 8389120 | tf_op jit(solution)/shard_map/while/body/eval_jaxpr/gather | solution.py:64
  152.9 3.8 %select_reduce_fusion.3 = f32[16,32,8]{1,2,0:T(8,128)S(1)} fusion(bf16[16,8,128,128]{3,2,1,0:T(8,128)(2,1)} %bitcast.90, pred[16,8,128]{2,1,0:T(8,128)(4,1)S(1)} %iota_compare_fusion.7, bf16[9,16,32,128]{3,2,1,0:T(8,128)(2,1)S(1)} %get-tuple-element.247, s32[]{:T(128)S(6)} %copy.464), kind=kOutput, calls=%fused_computation.6.clone.1 | convolution fusion | flops 135262208 | bytes 4358148 | tf_op jit(solution)/shard_map/while/body/eval_jaxpr/mqd,mkpd->mqkp/dot_general | solution.py:44
  156.9 1.4 dynamic_update_slice.5
  158.5 1.2 gather_fusion.1
  159.9 3.0 %gather_fusion = bf16[128,128,128]{2,1,0:T(8,128)(2,1)} fusion(bf16[32,128,128]{2,1,0:T(8,128)(2,1)S(1)} %get-tuple-element.248, s32[1024]{0:T(1024)S(1)} %pad_clamp_fusion.5), kind=kCustom, calls=%fused_computation.1.clone.1 | custom fusion | bytes 8389120 | tf_op jit(solution)/shard_map/while/body/eval_jaxpr/gather | solution.py:64
  162.9 3.8 %select_reduce_fusion.3 = f32[16,32,8]{1,2,0:T(8,128)S(1)} fusion(bf16[16,8,128,128]{3,2,1,0:T(8,128)(2,1)} %bitcast.90, pred[16,8,128]{2,1,0:T(8,128)(4,1)S(1)} %iota_compare_fusion.7, bf16[9,16,32,128]{3,2,1,0:T(8,128)(2,1)S(1)} %get-tuple-element.247, s32[]{:T(128)S(6)} %copy.464), kind=kOutput, calls=%fused_computation.6.clone.1 | convolution fusion | flops 135262208 | bytes 4358148 | tf_op jit(solution)/shard_map/while/body/eval_jaxpr/mqd,mkpd->mqkp/dot_general | solution.py:44
  166.9 1.4 dynamic_update_slice.5
  168.5 1.2 gather_fusion.1
  169.9 3.0 %gather_fusion = bf16[128,128,128]{2,1,0:T(8,128)(2,1)} fusion(bf16[32,128,128]{2,1,0:T(8,128)(2,1)S(1)} %get-tuple-element.248, s32[1024]{0:T(1024)S(1)} %pad_clamp_fusion.5), kind=kCustom, calls=%fused_computation.1.clone.1 | custom fusion | bytes 8389120 | tf_op jit(solution)/shard_map/while/body/eval_jaxpr/gather | solution.py:64
  173.0 3.8 %select_reduce_fusion.3 = f32[16,32,8]{1,2,0:T(8,128)S(1)} fusion(bf16[16,8,128,128]{3,2,1,0:T(8,128)(2,1)} %bitcast.90, pred[16,8,128]{2,1,0:T(8,128)(4,1)S(1)} %iota_compare_fusion.7, bf16[9,16,32,128]{3,2,1,0:T(8,128)(2,1)S(1)} %get-tuple-element.247, s32[]{:T(128)S(6)} %copy.464), kind=kOutput, calls=%fused_computation.6.clone.1 | convolution fusion | flops 135262208 | bytes 4358148 | tf_op jit(solution)/shard_map/while/body/eval_jaxpr/mqd,mkpd->mqkp/dot_general | solution.py:44
  176.9 1.4 dynamic_update_slice.5
  178.5 1.2 gather_fusion.1
  179.9 3.0 %gather_fusion = bf16[128,128,128]{2,1,0:T(8,128)(2,1)} fusion(bf16[32,128,128]{2,1,0:T(8,128)(2,1)S(1)} %get-tuple-element.248, s32[1024]{0:T(1024)S(1)} %pad_clamp_fusion.5), kind=kCustom, calls=%fused_computation.1.clone.1 | custom fusion | bytes 8389120 | tf_op jit(solution)/shard_map/while/body/eval_jaxpr/gather | solution.py:64
  183.0 3.8 %select_reduce_fusion.3 = f32[16,32,8]{1,2,0:T(8,128)S(1)} fusion(bf16[16,8,128,128]{3,2,1,0:T(8,128)(2,1)} %bitcast.90, pred[16,8,128]{2,1,0:T(8,128)(4,1)S(1)} %iota_compare_fusion.7, bf16[9,16,32,128]{3,2,1,0:T(8,128)(2,1)S(1)} %get-tuple-element.247, s32[]{:T(128)S(6)} %copy.464), kind=kOutput, calls=%fused_computation.6.clone.1 | convolution fusion | flops 135262208 | bytes 4358148 | tf_op jit(solution)/shard_map/while/body/eval_jaxpr/mqd,mkpd->mqkp/dot_general | solution.py:44
  187.0 1.4 dynamic_update_slice.5
  188.6 1.2 gather_fusion.1
  190.0 3.0 %gather_fusion = bf16[128,128,128]{2,1,0:T(8,128)(2,1)} fusion(bf16[32,128,128]{2,1,0:T(8,128)(2,1)S(1)} %get-tuple-element.248, s32[1024]{0:T(1024)S(1)} %pad_clamp_fusion.5), kind=kCustom, calls=%fused_computation.1.clone.1 | custom fusion | bytes 8389120 | tf_op jit(solution)/shard_map/while/body/eval_jaxpr/gather | solution.py:64
  193.0 3.8 %select_reduce_fusion.3 = f32[16,32,8]{1,2,0:T(8,128)S(1)} fusion(bf16[16,8,128,128]{3,2,1,0:T(8,128)(2,1)} %bitcast.90, pred[16,8,128]{2,1,0:T(8,128)(4,1)S(1)} %iota_compare_fusion.7, bf16[9,16,32,128]{3,2,1,0:T(8,128)(2,1)S(1)} %get-tuple-element.247, s32[]{:T(128)S(6)} %copy.464), kind=kOutput, calls=%fused_computation.6.clone.1 | convolution fusion | flops 135262208 | bytes 4358148 | tf_op jit(solution)/shard_map/while/body/eval_jaxpr/mqd,mkpd->mqkp/dot_general | solution.py:44
  197.0 1.4 dynamic_update_slice.5
  198.6 1.2 gather_fusion.1
  200.0 3.0 %gather_fusion = bf16[128,128,128]{2,1,0:T(8,128)(2,1)} fusion(bf16[32,128,128]{2,1,0:T(8,128)(2,1)S(1)} %get-tuple-element.248, s32[1024]{0:T(1024)S(1)} %pad_clamp_fusion.5), kind=kCustom, calls=%fused_computation.1.clone.1 | custom fusion | bytes 8389120 | tf_op jit(solution)/shard_map/while/body/eval_jaxpr/gather | solution.py:64
  203.0 3.8 %select_reduce_fusion.3 = f32[16,32,8]{1,2,0:T(8,128)S(1)} fusion(bf16[16,8,128,128]{3,2,1,0:T(8,128)(2,1)} %bitcast.90, pred[16,8,128]{2,1,0:T(8,128)(4,1)S(1)} %iota_compare_fusion.7, bf16[9,16,32,128]{3,2,1,0:T(8,128)(2,1)S(1)} %get-tuple-element.247, s32[]{:T(128)S(6)} %copy.464), kind=kOutput, calls=%fused_computation.6.clone.1 | convolution fusion | flops 135262208 | bytes 4358148 | tf_op jit(solution)/shard_map/while/body/eval_jaxpr/mqd,mkpd->mqkp/dot_general | solution.py:44
  207.0 1.4 dynamic_update_slice.5
  208.6 1.2 gather_fusion.1
  210.0 3.0 %gather_fusion = bf16[128,128,128]{2,1,0:T(8,128)(2,1)} fusion(bf16[32,128,128]{2,1,0:T(8,128)(2,1)S(1)} %get-tuple-element.248, s32[1024]{0:T(1024)S(1)} %pad_clamp_fusion.5), kind=kCustom, calls=%fused_computation.1.clone.1 | custom fusion | bytes 8389120 | tf_op jit(solution)/shard_map/while/body/eval_jaxpr/gather | solution.py:64
  213.1 3.8 %select_reduce_fusion.3 = f32[16,32,8]{1,2,0:T(8,128)S(1)} fusion(bf16[16,8,128,128]{3,2,1,0:T(8,128)(2,1)} %bitcast.90, pred[16,8,128]{2,1,0:T(8,128)(4,1)S(1)} %iota_compare_fusion.7, bf16[9,16,32,128]{3,2,1,0:T(8,128)(2,1)S(1)} %get-tuple-element.247, s32[]{:T(128)S(6)} %copy.464), kind=kOutput, calls=%fused_computation.6.clone.1 | convolution fusion | flops 135262208 | bytes 4358148 | tf_op jit(solution)/shard_map/while/body/eval_jaxpr/mqd,mkpd->mqkp/dot_general | solution.py:44
  217.0 1.4 dynamic_update_slice.5
  218.4 0.9 reshape_reshape.3
  220.0 3.5 %all-to-all-start.1 = ((f32[16,9,8]{1,2,0:T(8,128)}), f32[16,9,8]{1,2,0:T(8,128)S(1)}, u32[]{:S(2)}, u32[]{:S(2)}) async-start(f32[16,9,8]{1,2,0:T(8,128)} %copy.389), calls=%async_computation.1 | async-start | bytes 131072 | tf_op jit(solution)/shard_map/all_to_all | solution.py:152
  223.5 6.8 %all-to-all-done.1 = f32[16,9,8]{1,2,0:T(8,128)S(1)} async-done(((f32[16,9,8]{1,2,0:T(8,128)}), f32[16,9,8]{1,2,0:T(8,128)S(1)}, u32[]{:S(2)}, u32[]{:S(2)}) %all-to-all-start.1) | async-done | bytes 4640 | tf_op jit(solution)/shard_map/all_to_all | solution.py:152
  230.7 4.5 %gather_fusion.4 = f32[768]{0:T(1024)S(1)} fusion(f32[1152]{0:T(1024)S(1)} %reshape.307, s32[1024]{0:T(1024)S(1)} %pad_clamp_fusion.1), kind=kCustom, calls=%fused_computation.4 | custom fusion | bytes 9216 | tf_op jit(solution)/shard_map/jit(_take)/gather | solution.py:156
  (193 shorter events, 19.9 us)
Async XLA Ops:
  0.0 1.7 copy-start
  6.8 11.9 %copy-start.4 = (bf16[32,32,128]{2,1,0:T(8,128)(2,1)S(1)}, bf16[32,32,128]{2,1,0:T(8,128)(2,1)}, u32[]{:S(2)}) copy-start(bf16[32,32,128]{2,1,0:T(8,128)(2,1)} %param.10) | copy-start | bytes 786436
  11.2 36.4 %all-to-all-start = ((bf16[16,9,8]{1,2,0:T(8,128)(2,1)}), bf16[16,9,8]{1,2,0:T(8,128)(2,1)S(1)}, u32[]{:S(2)}, u32[]{:S(2)}) async-start(bf16[16,9,8]{1,2,0:T(8,128)(2,1)} %copy.383), calls=%async_computation | async-start | bytes 65536 | tf_op jit(solution)/shard_map/all_to_all | solution.py:142
  19.2 12.4 %copy-start.12 = (f32[4]{0:T(128)S(1)}, f32[4]{0:T(128)}, u32[]{:S(2)}) copy-start(f32[4]{0:T(128)} %param.17) | copy-start | bytes 52
  19.2 13.3 %copy-start.2 = (s32[32,128,128]{2,1,0:T(8,128)S(1)}, s32[32,128,128]{2,1,0:T(8,128)}, u32[]{:S(2)}) copy-start(s32[32,128,128]{2,1,0:T(8,128)} %param.15) | copy-start | bytes 6291460
  23.2 103.3 %collective-permute-start.14 = (bf16[1,9,32,128]{3,0,2,1:T(2,128)(2,1)}, bf16[1,9,32,128]{3,0,2,1:T(2,128)(2,1)}, u32[]{:S(2)}, u32[]{:S(2)}) collective-permute-start(bf16[1,9,32,128]{3,0,2,1:T(2,128)(2,1)} %get-tuple-element.164), channel_id=1, source_target_pairs={{0,15},{1,14},{2,13},{3,12},{4,11},{5,10},{6,9},{7,8},{8,7},{9,6},... | collective-permute-start | bytes 221192 | tf_op jit(solution)/shard_map/ppermute | solution.py:29
  27.5 98.1 %collective-permute-start.13 = (bf16[1,9,32,128]{3,0,2,1:T(2,128)(2,1)}, bf16[1,9,32,128]{3,0,2,1:T(2,128)(2,1)}, u32[]{:S(2)}, u32[]{:S(2)}) collective-permute-start(bf16[1,9,32,128]{3,0,2,1:T(2,128)(2,1)} %get-tuple-element.165), channel_id=1, source_target_pairs={{0,14},{1,15},{2,12},{3,13},{4,10},{5,11},{6,8},{7,9},{8,6},{9,7},... | collective-permute-start | bytes 221192 | tf_op jit(solution)/shard_map/ppermute | solution.py:29
  27.9 96.7 %collective-permute-start.12 = (bf16[1,9,32,128]{3,0,2,1:T(2,128)(2,1)}, bf16[1,9,32,128]{3,0,2,1:T(2,128)(2,1)}, u32[]{:S(2)}, u32[]{:S(2)}) collective-permute-start(bf16[1,9,32,128]{3,0,2,1:T(2,128)(2,1)} %get-tuple-element.166), channel_id=1, source_target_pairs={{0,13},{1,12},{2,15},{3,14},{4,9},{5,8},{6,11},{7,10},{8,5},{9,4},... | collective-permute-start | bytes 221192 | tf_op jit(solution)/shard_map/ppermute | solution.py:29
  31.0 92.6 %collective-permute-start.11 = (bf16[1,9,32,128]{3,0,2,1:T(2,128)(2,1)}, bf16[1,9,32,128]{3,0,2,1:T(2,128)(2,1)}, u32[]{:S(2)}, u32[]{:S(2)}) collective-permute-start(bf16[1,9,32,128]{3,0,2,1:T(2,128)(2,1)} %get-tuple-element.167), channel_id=1, source_target_pairs={{0,12},{1,13},{2,14},{3,15},{4,8},{5,9},{6,10},{7,11},{8,4},{9,5},... | collective-permute-start | bytes 221192 | tf_op jit(solution)/shard_map/ppermute | solution.py:29
  31.3 16.7 %collective-permute-start = (bf16[1,9,32,128]{3,0,2,1:T(2,128)(2,1)}, bf16[1,9,32,128]{3,0,2,1:T(2,128)(2,1)}, u32[]{:S(2)}, u32[]{:S(2)}) collective-permute-start(bf16[1,9,32,128]{3,0,2,1:T(2,128)(2,1)} %get-tuple-element.178), channel_id=1, source_target_pairs={{0,1},{1,0},{2,3},{3,2},{4,5},{5,4},{6,7},{7,6},{8,9},{9,8},{10,11... | collective-permute-start | bytes 221192 | tf_op jit(solution)/shard_map/ppermute | solution.py:29
  42.7 4.7 %copy-start.3 = (bf16[1,9,32,128]{3,0,2,1:T(2,128)(2,1)S(1)}, bf16[1,9,32,128]{3,0,2,1:T(2,128)(2,1)}, u32[]{:S(2)}) copy-start(bf16[1,9,32,128]{3,0,2,1:T(2,128)(2,1)} %get-tuple-element.179) | copy-start | bytes 221188
  47.3 19.2 %copy-start.11 = (bf16[1,9,32,128]{3,0,2,1:T(2,128)(2,1)S(1)}, bf16[1,9,32,128]{3,0,2,1:T(2,128)(2,1)}, u32[]{:S(2)}) copy-start(bf16[1,9,32,128]{3,0,2,1:T(2,128)(2,1)} %get-tuple-element.174) | copy-start | bytes 221188
  47.3 24.7 %copy-start.10 = (bf16[1,9,32,128]{3,0,2,1:T(2,128)(2,1)S(1)}, bf16[1,9,32,128]{3,0,2,1:T(2,128)(2,1)}, u32[]{:S(2)}) copy-start(bf16[1,9,32,128]{3,0,2,1:T(2,128)(2,1)} %get-tuple-element.173) | copy-start | bytes 221188
  47.3 30.9 %copy-start.9 = (bf16[1,9,32,128]{3,0,2,1:T(2,128)(2,1)S(1)}, bf16[1,9,32,128]{3,0,2,1:T(2,128)(2,1)}, u32[]{:S(2)}) copy-start(bf16[1,9,32,128]{3,0,2,1:T(2,128)(2,1)} %get-tuple-element.172) | copy-start | bytes 221188
  47.3 37.7 %copy-start.8 = (bf16[1,9,32,128]{3,0,2,1:T(2,128)(2,1)S(1)}, bf16[1,9,32,128]{3,0,2,1:T(2,128)(2,1)}, u32[]{:S(2)}) copy-start(bf16[1,9,32,128]{3,0,2,1:T(2,128)(2,1)} %get-tuple-element.171) | copy-start | bytes 221188
  47.3 47.3 %copy-start.7 = (bf16[1,9,32,128]{3,0,2,1:T(2,128)(2,1)S(1)}, bf16[1,9,32,128]{3,0,2,1:T(2,128)(2,1)}, u32[]{:S(2)}) copy-start(bf16[1,9,32,128]{3,0,2,1:T(2,128)(2,1)} %get-tuple-element.170) | copy-start | bytes 221188
  47.4 56.7 %copy-start.6 = (bf16[1,9,32,128]{3,0,2,1:T(2,128)(2,1)S(1)}, bf16[1,9,32,128]{3,0,2,1:T(2,128)(2,1)}, u32[]{:S(2)}) copy-start(bf16[1,9,32,128]{3,0,2,1:T(2,128)(2,1)} %get-tuple-element.169) | copy-start | bytes 221188
  47.6 65.7 %copy-start.5 = (bf16[1,9,32,128]{3,0,2,1:T(2,128)(2,1)S(1)}, bf16[1,9,32,128]{3,0,2,1:T(2,128)(2,1)}, u32[]{:S(2)}) copy-start(bf16[1,9,32,128]{3,0,2,1:T(2,128)(2,1)} %get-tuple-element.168) | copy-start | bytes 221188
  48.0 6.3 %collective-permute-start.1 = (bf16[1,9,32,128]{3,0,2,1:T(2,128)(2,1)}, bf16[1,9,32,128]{3,0,2,1:T(2,128)(2,1)S(1)}, u32[]{:S(2)}, u32[]{:S(2)}) collective-permute-start(bf16[1,9,32,128]{3,0,2,1:T(2,128)(2,1)} %get-tuple-element.177), channel_id=1, source_target_pairs={{0,2},{1,3},{2,0},{3,1},{4,6},{5,7},{6,4},{7,5},{8,10},{9,11},{10,... | collective-permute-start | bytes 221192 | tf_op jit(solution)/shard_map/ppermute | solution.py:29
  54.3 6.1 %collective-permute-start.2 = (bf16[1,9,32,128]{3,0,2,1:T(2,128)(2,1)}, bf16[1,9,32,128]{3,0,2,1:T(2,128)(2,1)S(1)}, u32[]{:S(2)}, u32[]{:S(2)}) collective-permute-start(bf16[1,9,32,128]{3,0,2,1:T(2,128)(2,1)} %get-tuple-element.176), channel_id=1, source_target_pairs={{0,3},{1,2},{2,1},{3,0},{4,7},{5,6},{6,5},{7,4},{8,11},{9,10},{10,... | collective-permute-start | bytes 221192 | tf_op jit(solution)/shard_map/ppermute | solution.py:29
  60.4 6.1 %collective-permute-start.3 = (bf16[1,9,32,128]{3,0,2,1:T(2,128)(2,1)}, bf16[1,9,32,128]{3,0,2,1:T(2,128)(2,1)S(1)}, u32[]{:S(2)}, u32[]{:S(2)}) collective-permute-start(bf16[1,9,32,128]{3,0,2,1:T(2,128)(2,1)} %get-tuple-element.175), channel_id=1, source_target_pairs={{0,4},{1,5},{2,6},{3,7},{4,0},{5,1},{6,2},{7,3},{8,12},{9,13},{10,... | collective-permute-start | bytes 221192 | tf_op jit(solution)/shard_map/ppermute | solution.py:29
  66.5 5.6 %collective-permute-start.4 = (bf16[1,9,32,128]{3,0,2,1:T(2,128)(2,1)S(1)}, bf16[1,9,32,128]{3,0,2,1:T(2,128)(2,1)S(1)}, u32[]{:S(2)}, u32[]{:S(2)}) collective-permute-start(bf16[1,9,32,128]{3,0,2,1:T(2,128)(2,1)S(1)} %copy-done.11), channel_id=1, source_target_pairs={{0,5},{1,4},{2,7},{3,6},{4,1},{5,0},{6,3},{7,2},{8,13},{9,12},{10,... | collective-permute-start | bytes 221192 | tf_op jit(solution)/shard_map/ppermute | solution.py:29
  72.0 6.2 %collective-permute-start.5 = (bf16[1,9,32,128]{3,0,2,1:T(2,128)(2,1)S(1)}, bf16[1,9,32,128]{3,0,2,1:T(2,128)(2,1)S(1)}, u32[]{:S(2)}, u32[]{:S(2)}) collective-permute-start(bf16[1,9,32,128]{3,0,2,1:T(2,128)(2,1)S(1)} %copy-done.10), channel_id=1, source_target_pairs={{0,6},{1,7},{2,4},{3,5},{4,2},{5,3},{6,0},{7,1},{8,14},{9,15},{10,... | collective-permute-start | bytes 221192 | tf_op jit(solution)/shard_map/ppermute | solution.py:29
  78.3 6.7 %collective-permute-start.6 = (bf16[1,9,32,128]{3,0,2,1:T(2,128)(2,1)S(1)}, bf16[1,9,32,128]{3,0,2,1:T(2,128)(2,1)S(1)}, u32[]{:S(2)}, u32[]{:S(2)}) collective-permute-start(bf16[1,9,32,128]{3,0,2,1:T(2,128)(2,1)S(1)} %copy-done.9), channel_id=1, source_target_pairs={{0,7},{1,6},{2,5},{3,4},{4,3},{5,2},{6,1},{7,0},{8,15},{9,14},{10,... | collective-permute-start | bytes 221192 | tf_op jit(solution)/shard_map/ppermute | solution.py:29
  85.0 9.7 %collective-permute-start.7 = (bf16[1,9,32,128]{3,0,2,1:T(2,128)(2,1)S(1)}, bf16[1,9,32,128]{3,0,2,1:T(2,128)(2,1)S(1)}, u32[]{:S(2)}, u32[]{:S(2)}) collective-permute-start(bf16[1,9,32,128]{3,0,2,1:T(2,128)(2,1)S(1)} %copy-done.8), channel_id=1, source_target_pairs={{0,8},{1,9},{2,10},{3,11},{4,12},{5,13},{6,14},{7,15},{8,0},{9,1},... | collective-permute-start | bytes 221192 | tf_op jit(solution)/shard_map/ppermute | solution.py:29
  94.7 9.4 %collective-permute-start.8 = (bf16[1,9,32,128]{3,0,2,1:T(2,128)(2,1)S(1)}, bf16[1,9,32,128]{3,0,2,1:T(2,128)(2,1)S(1)}, u32[]{:S(2)}, u32[]{:S(2)}) collective-permute-start(bf16[1,9,32,128]{3,0,2,1:T(2,128)(2,1)S(1)} %copy-done.7), channel_id=1, source_target_pairs={{0,9},{1,8},{2,11},{3,10},{4,13},{5,12},{6,15},{7,14},{8,1},{9,0},... | collective-permute-start | bytes 221192 | tf_op jit(solution)/shard_map/ppermute | solution.py:29
  104.1 9.2 %collective-permute-start.9 = (bf16[1,9,32,128]{3,0,2,1:T(2,128)(2,1)S(1)}, bf16[1,9,32,128]{3,0,2,1:T(2,128)(2,1)S(1)}, u32[]{:S(2)}, u32[]{:S(2)}) collective-permute-start(bf16[1,9,32,128]{3,0,2,1:T(2,128)(2,1)S(1)} %copy-done.6), channel_id=1, source_target_pairs={{0,10},{1,11},{2,8},{3,9},{4,14},{5,15},{6,12},{7,13},{8,2},{9,3},... | collective-permute-start | bytes 221192 | tf_op jit(solution)/shard_map/ppermute | solution.py:29
  113.3 10.3 %collective-permute-start.10 = (bf16[1,9,32,128]{3,0,2,1:T(2,128)(2,1)S(1)}, bf16[1,9,32,128]{3,0,2,1:T(2,128)(2,1)S(1)}, u32[]{:S(2)}, u32[]{:S(2)}) collective-permute-start(bf16[1,9,32,128]{3,0,2,1:T(2,128)(2,1)S(1)} %copy-done.5), channel_id=1, source_target_pairs={{0,11},{1,10},{2,9},{3,8},{4,15},{5,14},{6,13},{7,12},{8,3},{9,2},... | collective-permute-start | bytes 221192 | tf_op jit(solution)/shard_map/ppermute | solution.py:29
  127.4 0.8 copy-start.1
  220.0 10.4 %all-to-all-start.1 = ((f32[16,9,8]{1,2,0:T(8,128)}), f32[16,9,8]{1,2,0:T(8,128)S(1)}, u32[]{:S(2)}, u32[]{:S(2)}) async-start(f32[16,9,8]{1,2,0:T(8,128)} %copy.389), calls=%async_computation.1 | async-start | bytes 131072 | tf_op jit(solution)/shard_map/all_to_all | solution.py:152
  230.7 4.6 %copy-start.13 = (s32[32]{0:T(128)S(1)}, s32[32]{0:T(128)}, u32[]{:S(2)}) copy-start(s32[32]{0:T(128)} %param.12) | copy-start | bytes 388
